TPU v7x, 32 devices: a whole 2x2x4 slice. The times are simulated.
32 devices in a mesh: head: 4 (over x, core), tok: 8 (over z, y).
Axes of the slice: x: 2, y: 2, z: 4, core: 2. Of those that a mesh axis runs over, the one named last changes fastest.
Arguments:
- tokens: bfloat16 [512, 4096], P('tok'), may hold values from -6 to 6
- attn_gain: float32 [4096], replicated, may hold values from 0.5 to 1.5
- q_weight: bfloat16 [4096, 2048], P('tok', 'head'), may hold values from -0.09375 to 0.09375
- k_weight: bfloat16 [4096, 512], P('tok', 'head'), may hold values from -0.09375 to 0.09375
- v_weight: bfloat16 [4096, 512], P('tok', 'head'), may hold values from -0.09375 to 0.09375
- output_matrix: bfloat16 [2048, 4096], P('head', 'tok'), may hold values from -0.125 to 0.125
- key_cache: bfloat16 [64, 256, 512], P('tok', None, 'head'), may hold values from -400 to 400
- value_cache: bfloat16 [64, 256, 512], P('tok', None, 'head'), may hold values from -6 to 6
- cache_lengths: int32 [64], P('tok'), may hold values from 1 to 256
- row_request_index: int32 [8, 64], P('tok'), may hold values from 0 to 7, never falling along the last dimension, each value on 1 to 32 neighbouring positions
- ffn_gain: float32 [4096], replicated, may hold values from 0.5 to 1.5
- router_weight: bfloat16 [4096, 8], replicated, may hold values from -0.09375 to 0.09375
- routes: int32 [512, 2], P('tok'), may hold values from 0 to 7, all different within a row; in each aligned block of 64 rows (0 to 63, 64 to 127, ...) at most 18 rows name the same one
- gate_weight: bfloat16 [8, 4096, 14336], P('tok', None, 'head'), may hold values from -0.09375 to 0.09375
- up_weight: bfloat16 [8, 4096, 14336], P('tok', None, 'head'), may hold values from -0.09375 to 0.09375
- down_weight: bfloat16 [8, 14336, 4096], P('tok', None, 'head'), may hold values from -0.046875 to 0.046875
Outputs:
- layer_out: bfloat16 [512, 4096], P('tok', 'head')
Inputs may be any that keep to these rules, and one draw needn't show every extreme that they name: `row_request_index`: within the rows of one index of tok the request number never falls, every request has 1 to 32 rows, and one has exactly 32. `routes`: the two experts of a row differ; in the rows of one index of tok no expert is named more than 18 times, and that bound is reached.
All inputs are finite; a program needn't handle non-finite values.
Results may differ from a plain program's by a relative error of at most 0.012.
The roundings to bfloat16 on the way count: a program that leaves them out, or rounds other values in their place, can miss the bound.
Values may be sent and summed in bfloat16 or wider, within the bound.
A program may use at most 256 MiB of HBM per device.

v0:
```python
import jax
import jax.numpy as jnp
from jax import lax
from jax.sharding import PartitionSpec as P

D = 4096
HD = 128
Q_HEADS = 16
KV_HEADS = 4
EXPERTS = 8
CAP = 18
epsilon = 1e-05
rope_base = 1000000.0


def rms_norm(values, gain):
    values = values.astype(jnp.float32)
    factor = lax.rsqrt(jnp.mean(values * values, axis=-1, keepdims=True) + epsilon)
    return (values * factor * gain).astype(jnp.bfloat16)


def rotate(values, positions):
    half = values.shape[-1] // 2
    freqs = rope_base ** (-jnp.arange(half, dtype=jnp.float32) * 2.0 / values.shape[-1])
    angles = positions.astype(jnp.float32)[:, None] * freqs[None, :]
    cosine = jnp.concatenate([jnp.cos(angles), jnp.cos(angles)], axis=-1)[:, None, :]
    sine = jnp.concatenate([jnp.sin(angles), jnp.sin(angles)], axis=-1)[:, None, :]
    turned = jnp.concatenate([-values[..., half:], values[..., :half]], axis=-1)
    return values * cosine + turned * sine


def own_lengths(segment, lengths):
    match = segment[:, None] == jnp.arange(lengths.shape[0], dtype=jnp.int32)[None, :]
    return jnp.sum(jnp.where(match, lengths[None, :], 0), axis=1)


def row_positions(segment, lengths):
    count = segment.shape[0]
    order = jnp.arange(count, dtype=jnp.int32)
    before = jnp.sum((segment[None, :] < segment[:, None]).astype(jnp.int32), axis=1)
    return own_lengths(segment, lengths) + order - before


def attend(queries, new_keys, new_values, key_cache, value_cache, segment, lengths):
    count, kv_local, group, size = queries.shape
    requests, slots, _ = key_cache.shape
    keys = jnp.concatenate([key_cache.reshape(requests * slots, kv_local, size), new_keys], axis=0)
    values = jnp.concatenate(
        [value_cache.reshape(requests * slots, kv_local, size), new_values], axis=0
    )
    slot_index = jnp.arange(requests * slots, dtype=jnp.int32)
    slot_request = slot_index // slots
    slot_place = slot_index % slots
    limit = own_lengths(segment, lengths)
    cache_valid = (slot_request[None, :] == segment[:, None]) & (
        slot_place[None, :] < limit[:, None]
    )
    order = jnp.arange(count, dtype=jnp.int32)
    new_valid = (segment[None, :] == segment[:, None]) & (order[None, :] <= order[:, None])
    allowed = jnp.concatenate([cache_valid, new_valid], axis=1)
    scores = jnp.einsum("rhgd,khd->hgrk", queries, keys, preferred_element_type=jnp.float32)
    scores = scores / jnp.sqrt(jnp.float32(size))
    scores = jnp.where(allowed[None, None], scores, jnp.float32(-1e30))
    highest = jnp.max(scores, axis=-1, keepdims=True)
    weights = jnp.exp(scores - highest)
    probs = (weights / jnp.sum(weights, axis=-1, keepdims=True)).astype(jnp.bfloat16)
    result = jnp.einsum("hgrk,khd->rhgd", probs, values, preferred_element_type=jnp.float32)
    return result.astype(jnp.bfloat16).reshape(count, kv_local * group * size)


def slot_table(chosen):
    flat = chosen.reshape(-1)
    onehot = (flat[:, None] == jnp.arange(EXPERTS, dtype=jnp.int32)[None, :]).astype(jnp.int32)
    earlier = jnp.cumsum(onehot, axis=0) - onehot
    place = jnp.sum(earlier * onehot, axis=1)
    return flat * CAP + place


def fill_slots(normed_rows, places):
    copies = normed_rows[jnp.arange(places.shape[0], dtype=jnp.int32) // 2]
    return jnp.zeros((EXPERTS * CAP, normed_rows.shape[1]), jnp.bfloat16).at[places].set(copies)


def gate_shares(normed_rows, router_weight, chosen):
    logits = jnp.dot(normed_rows, router_weight, preferred_element_type=jnp.float32)
    match = chosen[:, :, None] == jnp.arange(EXPERTS, dtype=jnp.int32)[None, None, :]
    picked = jnp.sum(jnp.where(match, logits[:, None, :], jnp.float32(0.0)), axis=-1)
    return jax.nn.sigmoid(picked - picked[:, ::-1])


def shards(
    tokens,
    attn_gain,
    q_weight,
    k_weight,
    v_weight,
    output_matrix,
    key_cache,
    value_cache,
    cache_lengths,
    row_request_index,
    ffn_gain,
    router_weight,
    routes,
    gate_weight,
    up_weight,
    down_weight,
):
    count = tokens.shape[0]
    group = Q_HEADS // KV_HEADS
    normed = rms_norm(tokens, attn_gain)
    q_full, k_full, v_full, o_full = (
        lax.all_gather(q_weight, "tok", axis=0, tiled=True),
        lax.all_gather(k_weight, "tok", axis=0, tiled=True),
        lax.all_gather(v_weight, "tok", axis=0, tiled=True),
        lax.all_gather(output_matrix, "tok", axis=1, tiled=True),
    )
    kv_local = k_full.shape[1] // HD
    queries = jnp.dot(normed, q_full, preferred_element_type=jnp.float32)
    keys_new = jnp.dot(normed, k_full, preferred_element_type=jnp.float32)
    values_new = jnp.dot(normed, v_full, preferred_element_type=jnp.float32)
    segment = row_request_index[0]
    positions = row_positions(segment, cache_lengths)
    queries = rotate(queries.reshape(count, kv_local * group, HD), positions).astype(jnp.bfloat16)
    queries = queries.reshape(count, kv_local, group, HD)
    keys_new = rotate(keys_new.reshape(count, kv_local, HD), positions).astype(jnp.bfloat16)
    values_new = values_new.astype(jnp.bfloat16).reshape(count, kv_local, HD)
    attn = attend(queries, keys_new, values_new, key_cache, value_cache, segment, cache_lengths)
    partial_mix = jnp.dot(attn, o_full, preferred_element_type=jnp.float32)
    mixed = lax.psum(partial_mix, "head")
    hidden_activation = tokens.astype(jnp.float32) + mixed
    normed_ffn = rms_norm(hidden_activation, ffn_gain)
    shares = gate_shares(normed_ffn, router_weight, routes)
    places = slot_table(routes)
    buffer = fill_slots(normed_ffn, places)
    owners = lax.axis_size("tok")
    slices = owners // EXPERTS
    quarter = down_weight.shape[2]
    head_index = lax.axis_index("head")
    outgoing = jnp.broadcast_to(
        buffer.reshape(EXPERTS, 1, CAP, D), (EXPERTS, slices, CAP, D)
    ).reshape(owners, CAP, D)
    arrived = lax.all_to_all(outgoing, "tok", split_axis=0, concat_axis=0, tiled=True)
    active = jnp.einsum("tcd,df->tcf", arrived, gate_weight[0], preferred_element_type=jnp.float32)
    linear = jnp.einsum("tcd,df->tcf", arrived, up_weight[0], preferred_element_type=jnp.float32)
    hidden = (jax.nn.silu(active) * linear).astype(jnp.bfloat16)
    hidden_all = lax.all_gather(hidden, "head", axis=2, tiled=True)
    output = jnp.einsum(
        "tcf,fd->tcd", hidden_all, down_weight[0], preferred_element_type=jnp.float32
    )
    layer_results = output.astype(jnp.bfloat16)
    returned = lax.all_to_all(layer_results, "tok", split_axis=0, concat_axis=0, tiled=True)
    summed = jnp.sum(returned.reshape(EXPERTS, slices, CAP, quarter).astype(jnp.float32), axis=1)
    summed = summed.reshape(EXPERTS * CAP, quarter)
    picked = jnp.take(summed, places, axis=0).reshape(count, 2, quarter)
    mixture = jnp.sum(shares[:, :, None] * picked, axis=1)
    residual = lax.dynamic_slice_in_dim(hidden_activation, head_index * quarter, quarter, 1)
    return (residual + mixture).astype(jnp.bfloat16)


def solution(mesh):
    in_specs = (
        P("tok", None),
        P(),
        P("tok", "head"),
        P("tok", "head"),
        P("tok", "head"),
        P("head", "tok"),
        P("tok", None, "head"),
        P("tok", None, "head"),
        P("tok"),
        P("tok", None),
        P(),
        P(),
        P("tok", None),
        P("tok", None, "head"),
        P("tok", None, "head"),
        P("tok", None, "head"),
    )
    out_specs = P("tok", "head")
    return jax.shard_map(shards, mesh=mesh, in_specs=in_specs, out_specs=out_specs, check_vma=False)
```

profile of v0, /device:TPU:0, one launch (start us, length us, event | category | flops | bytes accessed | tf_op | source)
XLA Modules:
  0.0 441.3 jit_solution(15756063312826419682)
XLA Ops:
  6.6 0.7 all-gather.6.cloned.1.call-update
  7.3 0.7 all-gather.8.cloned.1.call-update
  8.1 0.7 all-gather.10.cloned.1.call-update
  9.4 0.8 copy.36
  10.3 0.7 broadcast_multiply_fusion
  11.5 0.9 convert_reduce_fusion
  12.4 0.8 select_reduce_fusion.2
  13.2 1.2 fusion.21
  14.4 0.8 fusion.42
  15.7 36.7 %all-gather.6.cloned.1.call-done = bf16[4096,128]{1,0:T(8,128)(2,1)} async-done(((bf16[512,128]{1,0:T(8,128)(2,1)}), bf16[4096,128]{1,0:T(8,128)(2,1)}) %all-gather.6.cloned.1.call-update) | async-done | bytes 1048592 | tf_op jit(solution)/shard_map/all_gather | solution.py:115
  52.4 1.6 fusion.20
  54.0 39.5 %all-gather.8.cloned.1.call-done = bf16[4096,128]{1,0:T(8,128)(2,1)} async-done(((bf16[512,128]{1,0:T(8,128)(2,1)}), bf16[4096,128]{1,0:T(8,128)(2,1)}) %all-gather.8.cloned.1.call-update) | async-done | bytes 1048592 | tf_op jit(solution)/shard_map/all_gather | solution.py:114
  93.4 1.6 fusion.57
  95.2 72.5 %all-gather.10.cloned.1.call-done = bf16[4096,512]{1,0:T(8,128)(2,1)} async-done(((bf16[512,512]{1,0:T(8,128)(2,1)}), bf16[4096,512]{1,0:T(8,128)(2,1)}) %all-gather.10.cloned.1.call-update) | async-done | bytes 4194320 | tf_op jit(solution)/shard_map/all_gather | solution.py:113
  167.8 3.1 fusion.55
  171.2 0.7 fusion.60
  172.9 70.0 %all-gather.12.cloned.1.call-done = bf16[512,4096]{1,0:T(8,128)(2,1)} async-done(((bf16[512,512]{1,0:T(8,128)(2,1)}), bf16[512,4096]{1,0:T(8,128)(2,1)}) %all-gather.12.cloned.1.call-update) | async-done | bytes 4194320 | tf_op jit(solution)/shard_map/all_gather | solution.py:116
  243.0 4.0 fusion.33
  247.3 34.1 %all-reduce.2.cloned.1.call-done = f32[64,4096]{1,0:T(8,128)} async-done(((f32[64,4096]{1,0:T(8,128)}), f32[64,4096]{1,0:T(8,128)}) %all-reduce.2.cloned.1.call-update) | async-done | bytes 1048592 | tf_op jit(solution)/shard_map/psum | solution.py:130
  281.4 1.5 multiply_reduce_fusion
  283.1 6.2 %scatter_custom_fusion = bf16[144,4096]{1,0:T(8,128)(2,1)} fusion(s32[128]{0:T(128)S(1)} %fusion.52, bf16[64,4096]{1,0:T(8,128)(2,1)S(1)} %multiply_convert_fusion, s32[1024]{0:T(1024)S(1)} %pad_clamp_fusion.1, bf16[]{:T(256)} %constant.104.clone.1), kind=kCustom, calls=%fused_computation.29 | custom fusion | bytes 1179650 | tf_op jit(solution)/shard_map/scatter | solution.py:81
  289.2 1.4 reshape_reshape.3
  290.7 41.9 %all_to_all.10 = bf16[8,18,4096]{2,1,0:T(8,128)(2,1)S(1)} all-to-all(bf16[8,18,4096]{2,1,0:T(8,128)(2,1)S(1)} %reshape_reshape.3), channel_id=1, replica_groups=mesh['head'=4,'tok'=8] {'tok'}, dimensions={0} | all-to-all | bytes 2359296 | tf_op jit(solution)/shard_map/all_to_all | solution.py:143
  332.6 12.5 %fusion.4 = f32[8,18,3584]{2,1,0:T(8,128)S(1)} fusion(bf16[8,18,4096]{2,1,0:T(8,128)(2,1)S(1)} %all_to_all.10, bf16[1,4096,3584]{2,1,0:T(8,128)(2,1)} %param.29), kind=kOutput, calls=%fused_computation.7 | convolution fusion | flops 4227858432 | bytes 32604160 | tf_op jit(solution)/shard_map/tcd,df->tcf/dot_general | solution.py:144
  345.1 13.5 %fusion.9 = bf16[8,18,3584]{2,1,0:T(8,128)(2,1)} fusion(bf16[8,18,4096]{2,1,0:T(8,128)(2,1)S(1)} %all_to_all.10, bf16[1,4096,3584]{2,1,0:T(8,128)(2,1)} %param.30, f32[8,18,3584]{2,1,0:T(8,128)S(1)} %fusion.4), kind=kOutput, calls=%fused_computation.10 | convolution fusion | flops 4230955008 | bytes 33636352 | tf_op jit(solution)/shard_map/tcd,df->tcf/dot_general | solution.py:145
  359.0 40.4 %all-gather.14.cloned.1.call-done = bf16[8,18,14336]{2,1,0:T(8,128)(2,1)} async-done(((bf16[8,18,3584]{2,1,0:T(8,128)(2,1)}), bf16[8,18,14336]{2,1,0:T(8,128)(2,1)}) %all-gather.14.cloned.1.call-update) | async-done | bytes 4128784 | tf_op jit(solution)/shard_map/all_gather | solution.py:147
  399.4 14.7 %fusion.15 = bf16[8,18,1024]{2,1,0:T(8,128)(2,1)} fusion(bf16[8,18,14336]{2,1,0:T(8,128)(2,1)} %all-gather.14.cloned.1.call-done, bf16[1,14336,1024]{2,1,0:T(8,128)(2,1)} %param.31), kind=kOutput, calls=%fused_computation.20 | convolution fusion | flops 4228005888 | bytes 33783808 | tf_op jit(solution)/shard_map/tcf,fd->tcd/dot_general | solution.py:148
  414.1 5.5 %all-to-all-start.1 = ((bf16[8,18,1024]{2,1,0:T(8,128)(2,1)}), bf16[8,18,1024]{2,1,0:T(8,128)(2,1)S(1)}, u32[]{:S(2)}, u32[]{:S(2)}) async-start(bf16[8,18,1024]{2,1,0:T(8,128)(2,1)} %fusion.15), calls=%async_computation.1 | async-start | bytes 786432 | tf_op jit(solution)/shard_map/all_to_all | solution.py:152
  420.0 11.7 %all-to-all-done.1 = bf16[8,18,1024]{2,1,0:T(8,128)(2,1)S(1)} async-done(((bf16[8,18,1024]{2,1,0:T(8,128)(2,1)}), bf16[8,18,1024]{2,1,0:T(8,128)(2,1)S(1)}, u32[]{:S(2)}, u32[]{:S(2)}) %all-to-all-start.1) | async-done | bytes 294944 | tf_op jit(solution)/shard_map/all_to_all | solution.py:152
  431.8 0.8 gather_fusion
  432.9 0.8 multiply_reduce_fusion.1
  433.8 0.7 add_convert_fusion
  (64 shorter events, 4.9 us)
Async XLA Ops:
  6.5 413.1 %copy-start = (bf16[4096,8]{0,1:T(8,128)(2,1)S(1)}, bf16[4096,8]{0,1:T(8,128)(2,1)}, u32[]{:S(2)}) copy-start(bf16[4096,8]{0,1:T(8,128)(2,1)} %param.27) | copy-start | bytes 196612
  6.5 8.9 %copy-start.5 = (s32[1,64]{1,0:T(1,128)S(1)}, s32[1,64]{1,0:T(1,128)}, u32[]{:S(2)}) copy-start(s32[1,64]{1,0:T(1,128)} %param.25) | copy-start | bytes 772
  6.5 45.8 %copy-start.1 = (bf16[64,4096]{1,0:T(8,128)(2,1)S(1)}, bf16[64,4096]{1,0:T(8,128)(2,1)}, u32[]{:S(2)}) copy-start(bf16[64,4096]{1,0:T(8,128)(2,1)} %param.16) | copy-start | bytes 1572868
  6.5 45.8 %copy-start.2 = (f32[4096]{0:T(1024)S(1)}, f32[4096]{0:T(1024)}, u32[]{:S(2)}) copy-start(f32[4096]{0:T(1024)} %param.17) | copy-start | bytes 49156
  6.5 45.8 %all-gather.6.cloned.1.call-start = ((), (), s32[]{:S(2)}) async-start(), calls=%async_computation.2 | async-start | bytes 1179648 | tf_op jit(solution)/shard_map/all_gather | solution.py:115
  7.3 86.2 %all-gather.8.cloned.1.call-start = ((), (), s32[]{:S(2)}) async-start(), calls=%async_computation.3 | async-start | bytes 1179648 | tf_op jit(solution)/shard_map/all_gather | solution.py:114
  8.0 159.7 %all-gather.10.cloned.1.call-start = ((), (), s32[]{:S(2)}) async-start(), calls=%async_computation.4 | async-start | bytes 4718592 | tf_op jit(solution)/shard_map/all_gather | solution.py:113
  8.8 234.2 %all-gather.12.cloned.1.call-start = ((), (), s32[]{:S(2)}) async-start(), calls=%async_computation.5 | async-start | bytes 4718592 | tf_op jit(solution)/shard_map/all_gather | solution.py:116
  9.3 272.1 %all-reduce.2.cloned.1.call-start = ((), (), s32[]{:S(2)}) async-start(), calls=%async_computation.6 | async-start | bytes 2097152 | tf_op jit(solution)/shard_map/psum | solution.py:130
  95.2 76.0 %copy-start.6 = (bf16[8,256,128]{2,1,0:T(8,128)(2,1)S(1)}, bf16[8,256,128]{2,1,0:T(8,128)(2,1)}, u32[]{:S(2)}) copy-start(bf16[8,256,128]{2,1,0:T(8,128)(2,1)} %param.22) | copy-start | bytes 1572868
  171.2 1.1 copy-start.7
  247.0 35.9 %copy-start.3 = (f32[4096]{0:T(1024)S(1)}, f32[4096]{0:T(1024)}, u32[]{:S(2)}) copy-start(f32[4096]{0:T(1024)} %param.26) | copy-start | bytes 49156
  247.0 152.4 %all-gather.14.cloned.1.call-start = ((), (), s32[]{:S(2)}) async-start(), calls=%async_computation.7 | async-start | bytes 6881280 | tf_op jit(solution)/shard_map/all_gather | solution.py:147
  345.1 13.7 %copy-start.4 = (s32[64,2]{0,1:T(2,128)S(1)}, s32[64,2]{0,1:T(2,128)}, u32[]{:S(2)}) copy-start(s32[64,2]{0,1:T(2,128)} %param.28) | copy-start | bytes 1540
  414.1 17.6 %all-to-all-start.1 = ((bf16[8,18,1024]{2,1,0:T(8,128)(2,1)}), bf16[8,18,1024]{2,1,0:T(8,128)(2,1)S(1)}, u32[]{:S(2)}, u32[]{:S(2)}) async-start(bf16[8,18,1024]{2,1,0:T(8,128)(2,1)} %fusion.15), calls=%async_computation.1 | async-start | bytes 786432 | tf_op jit(solution)/shard_map/all_to_all | solution.py:152
Sparse Core Ops, SparseCore 0:
  9.5 42.8 all-gather.5
  54.5 38.8 all-gather.7
  95.6 72.1 all-gather.9
  169.7 73.2 all-gather.11
  247.1 34.2 all-reduce.1
  358.7 40.6 all-gather.13
where the time goes:
time: 442 us; the launch traced here: 441 us
  waiting for transfers between devices  308 us (70%)
  matrix products  52.4 us (12%)
  blocking collectives  41.9 us (9%)
  between operations  13.8 us (3%)
  local copies, waits for them, and re-layouts  10.5 us (2%)
  other arithmetic  9.38 us (2%)
  starting transfers between devices  5.74 us (1%)
    all_gather x1, waiting for transfers between devices, shards(): lax.all_gather(q_weight, 'tok', axis=0, tiled=True)  72.5 us
    all_gather x1, waiting for transfers between devices, shards(): lax.all_gather(output_matrix, 'tok', axis=1, tiled=True)  70 us
    all_to_all x1, blocking collectives, shards(): lax.all_to_all(outgoing, 'tok', split_axis=0, concat_axis=0, tiled=True)  41.9 us
    all_gather x1, waiting for transfers between devices, shards(): hidden_all = lax.all_gather(hidden, 'head', axis=2, tiled=True)  40.4 us
    all_gather x1, waiting for transfers between devices, shards(): lax.all_gather(k_weight, 'tok', axis=0, tiled=True)  39.5 us
    all_gather x1, waiting for transfers between devices, shards(): lax.all_gather(v_weight, 'tok', axis=0, tiled=True)  36.7 us
    psum x1, waiting for transfers between devices, shards(): mixed = lax.psum(partial_mix, 'head')  34.1 us
    dot_general x1, matrix products, shards(): jnp.einsum('tcf,fd->tcd', hidden_all, down_weight[0], preferred_element_t...  14.7 us
  transfers between devices with their start and end apart: 7, of which 7 were waited for; matrix products, arithmetic and copies ran while one was open for 4% of the time, Pallas kernels for 0%

commit v1 on v0

--- a/solution.py
+++ b/solution.py
@@ -106,6 +106,21 @@
     up_weight,
     down_weight,
 ):
+
+    def leaf_start(block_here, which_axis):
+        carry = jax.lax.psum(1, axis_name=which_axis)
+        s_next = jax.lax.axis_index(which_axis)
+        block_out, plain = (carry, s_next)
+        next_value, y1 = (block_here, 1)
+        while y1 < block_out:
+            small = tuple(((idx, idx ^ y1) for idx in range(block_out)))
+            r1 = jax.lax.ppermute(next_value, axis_name=which_axis, perm=small)
+            tmp = jnp.concatenate([next_value, r1], axis=1)
+            now = jnp.concatenate([r1, next_value], axis=1)
+            next_value = jnp.where(plain & y1 == 0, tmp, now)
+            y1 = 2 * y1
+        return next_value
+
     count = tokens.shape[0]
     group = Q_HEADS // KV_HEADS
     normed = rms_norm(tokens, attn_gain)
@@ -113,7 +128,7 @@
         lax.all_gather(q_weight, "tok", axis=0, tiled=True),
         lax.all_gather(k_weight, "tok", axis=0, tiled=True),
         lax.all_gather(v_weight, "tok", axis=0, tiled=True),
-        lax.all_gather(output_matrix, "tok", axis=1, tiled=True),
+        leaf_start(output_matrix, "tok"),
     )
     kv_local = k_full.shape[1] // HD
     queries = jnp.dot(normed, q_full, preferred_element_type=jnp.float32)

time: 442 us -> 462 us (1.045)
  waiting for transfers between devices: 308 us -> 315 us
  starting transfers between devices: 5.74 us -> 12.7 us
    all_gather x1, waiting for transfers between devices: 36.7 us -> 115 us  [shards(): lax.all_gather(v_weight, 'tok', axis=0, tiled=True)]
    all_gather x1 -> x0, waiting for transfers between devices: 70 us -> none  [shards(): lax.all_gather(output_matrix, 'tok', axis=1, tiled=True)]
    ppermute x0 -> x3, waiting for transfers between devices: none -> 39.5 us  [leaf_start(): r1 = jax.lax.ppermute(next_value, axis_name=which_axis, perm=small)]
    all_gather x1, waiting for transfers between devices: 39.5 us -> 0.01 us  [shards(): lax.all_gather(k_weight, 'tok', axis=0, tiled=True)]
    ppermute x0 -> x3, starting transfers between devices: none -> 6.99 us  [leaf_start(): r1 = jax.lax.ppermute(next_value, axis_name=which_axis, perm=small)]
  transfers between devices with their start and end apart: 7 -> 9, of which waited for: 7 -> 7; matrix products, arithmetic and copies ran while one was open for 4% -> 4% of each run, Pallas kernels for 0% -> 0%
where the time goes in v1:
time: 462 us; the launch traced here: 461 us
  waiting for transfers between devices  315 us (68%)
  matrix products  54.2 us (12%)
  blocking collectives  41.9 us (9%)
  between operations  13.5 us (3%)
  other arithmetic  13 us (3%)
  starting transfers between devices  12.7 us (3%)
  local copies, waits for them, and re-layouts  10.5 us (2%)
    all_gather x1, waiting for transfers between devices, shards(): lax.all_gather(v_weight, 'tok', axis=0, tiled=True)  115 us
    all_gather x1, waiting for transfers between devices, shards(): lax.all_gather(q_weight, 'tok', axis=0, tiled=True)  72.6 us
    all_to_all x1, blocking collectives, shards(): lax.all_to_all(outgoing, 'tok', split_axis=0, concat_axis=0, tiled=True)  41.9 us
    all_gather x1, waiting for transfers between devices, shards(): hidden_all = lax.all_gather(hidden, 'head', axis=2, tiled=True)  40.4 us
    ppermute x3, waiting for transfers between devices, leaf_start(): r1 = jax.lax.ppermute(next_value, axis_name=which_axis, perm=small)  39.5 us
    psum x1, waiting for transfers between devices, shards(): mixed = lax.psum(partial_mix, 'head')  34.2 us
    dot_general x1, matrix products, shards(): jnp.einsum('tcf,fd->tcd', hidden_all, down_weight[0], preferred_element_t...  14.7 us
    dot_general x1, matrix products, shards(): jnp.einsum('tcd,df->tcf', arrived, up_weight[0], preferred_element_type=j...  13.5 us
  transfers between devices with their start and end apart: 9, of which 7 were waited for; matrix products, arithmetic and copies ran while one was open for 4% of the time, Pallas kernels for 0%

profile of v1, /device:TPU:0, one launch (start us, length us, event | category | flops | bytes accessed | tf_op | source)
XLA Modules:
  0.0 461.1 jit_solution(6740471846133680977)
XLA Ops:
  6.5 0.7 all-gather.7.cloned.1.call-update
  8.8 3.0 collective-permute-start
  11.8 0.8 copy.36
  12.7 0.9 convert_reduce_fusion
  13.7 0.8 select_reduce_fusion.2
  14.4 1.3 fusion.28
  16.4 0.8 fusion.48
  17.3 8.1 %collective-permute-done = bf16[512,512]{1,0:T(8,128)(2,1)S(1)} collective-permute-done((bf16[512,512]{1,0:T(8,128)(2,1)}, bf16[512,512]{1,0:T(8,128)(2,1)S(1)}, u32[]{:S(2)}, u32[]{:S(2)}) %collective-permute-start) | collective-permute-done | bytes 524320 | tf_op jit(solution)/shard_map/ppermute | solution.py:117
  25.4 1.5 maximum_select_fusion.3
  26.9 1.9 collective-permute-start.1
  29.6 31.4 %collective-permute-done.1 = bf16[512,1024]{1,0:T(8,128)(2,1)S(1)} collective-permute-done((bf16[512,1024]{1,0:T(8,128)(2,1)S(1)}, bf16[512,1024]{1,0:T(8,128)(2,1)S(1)}, u32[]{:S(2)}, u32[]{:S(2)}) %collective-permute-start.1) | collective-permute-done | bytes 1048608 | tf_op jit(solution)/shard_map/ppermute | solution.py:117
  61.1 2.1 maximum_select_fusion.2
  63.2 2.1 collective-permute-start.2
  65.3 1.6 fusion.64
  67.0 114.6 %all-gather.5.cloned.1.call-done = bf16[4096,128]{1,0:T(8,128)(2,1)} async-done(((bf16[512,128]{1,0:T(8,128)(2,1)}), bf16[4096,128]{1,0:T(8,128)(2,1)}) %all-gather.5.cloned.1.call-update) | async-done | bytes 1048592 | tf_op jit(solution)/shard_map/all_gather | solution.py:130
  181.6 1.6 fusion.27
  183.3 72.6 %all-gather.9.cloned.1.call-done = bf16[4096,512]{1,0:T(8,128)(2,1)} async-done(((bf16[512,512]{1,0:T(8,128)(2,1)}), bf16[4096,512]{1,0:T(8,128)(2,1)}) %all-gather.9.cloned.1.call-update) | async-done | bytes 4194320 | tf_op jit(solution)/shard_map/all_gather | solution.py:128
  255.9 3.1 fusion.62
  261.1 5.9 %fusion.12 = f32[64,4096]{1,0:T(8,128)} fusion(bf16[512,2048]{1,0:T(8,128)(2,1)} %collective-permute-done.2, bf16[512,2048]{1,0:T(8,128)(2,1)} %maximum_select_fusion.2, pred[]{:T(512)S(6)} %eq.95, bf16[8,8,4,128]{3,2,1,0:T(4,128)(2,1)S(1)} %bitcast.105), kind=kOutput, calls=%fused_computation.13 | convolution fusion | flops 287309824 | bytes 5308417 | tf_op jit(solution)/shard_map/dot_general | solution.py:144
  267.2 34.2 %all-reduce.2.cloned.1.call-done = f32[64,4096]{1,0:T(8,128)} async-done(((f32[64,4096]{1,0:T(8,128)}), f32[64,4096]{1,0:T(8,128)}) %all-reduce.2.cloned.1.call-update) | async-done | bytes 1048592 | tf_op jit(solution)/shard_map/psum | solution.py:145
  301.5 1.5 multiply_reduce_fusion
  303.1 6.2 %scatter_custom_fusion = bf16[144,4096]{1,0:T(8,128)(2,1)} fusion(s32[128]{0:T(128)S(1)} %fusion.58, bf16[64,4096]{1,0:T(8,128)(2,1)S(1)} %multiply_convert_fusion, s32[1024]{0:T(1024)S(1)} %pad_clamp_fusion.1, bf16[]{:T(256)} %constant.111.clone.1), kind=kCustom, calls=%fused_computation.39 | custom fusion | bytes 1179650 | tf_op jit(solution)/shard_map/scatter | solution.py:81
  309.3 1.4 reshape_reshape.3
  310.8 41.9 %all_to_all.10 = bf16[8,18,4096]{2,1,0:T(8,128)(2,1)S(1)} all-to-all(bf16[8,18,4096]{2,1,0:T(8,128)(2,1)S(1)} %reshape_reshape.3), channel_id=1, replica_groups=mesh['head'=4,'tok'=8] {'tok'}, dimensions={0} | all-to-all | bytes 2359296 | tf_op jit(solution)/shard_map/all_to_all | solution.py:158
  352.6 12.5 %fusion.4 = f32[8,18,3584]{2,1,0:T(8,128)S(1)} fusion(bf16[8,18,4096]{2,1,0:T(8,128)(2,1)S(1)} %all_to_all.10, bf16[1,4096,3584]{2,1,0:T(8,128)(2,1)} %param.29), kind=kOutput, calls=%fused_computation.7 | convolution fusion | flops 4227858432 | bytes 32604160 | tf_op jit(solution)/shard_map/tcd,df->tcf/dot_general | solution.py:159
  365.2 13.5 %fusion.9 = bf16[8,18,3584]{2,1,0:T(8,128)(2,1)} fusion(bf16[8,18,4096]{2,1,0:T(8,128)(2,1)S(1)} %all_to_all.10, bf16[1,4096,3584]{2,1,0:T(8,128)(2,1)} %param.30, f32[8,18,3584]{2,1,0:T(8,128)S(1)} %fusion.4), kind=kOutput, calls=%fused_computation.10 | convolution fusion | flops 4230955008 | bytes 33636352 | tf_op jit(solution)/shard_map/tcd,df->tcf/dot_general | solution.py:160
  379.1 40.4 %all-gather.11.cloned.1.call-done = bf16[8,18,14336]{2,1,0:T(8,128)(2,1)} async-done(((bf16[8,18,3584]{2,1,0:T(8,128)(2,1)}), bf16[8,18,14336]{2,1,0:T(8,128)(2,1)}) %all-gather.11.cloned.1.call-update) | async-done | bytes 4128784 | tf_op jit(solution)/shard_map/all_gather | solution.py:162
  419.5 14.7 %fusion.22 = bf16[8,18,1024]{2,1,0:T(8,128)(2,1)} fusion(bf16[8,18,14336]{2,1,0:T(8,128)(2,1)} %all-gather.11.cloned.1.call-done, bf16[1,14336,1024]{2,1,0:T(8,128)(2,1)} %param.31), kind=kOutput, calls=%fused_computation.29 | convolution fusion | flops 4228005888 | bytes 33783808 | tf_op jit(solution)/shard_map/tcf,fd->tcd/dot_general | solution.py:163
  434.2 5.5 %all-to-all-start.1 = ((bf16[8,18,1024]{2,1,0:T(8,128)(2,1)}), bf16[8,18,1024]{2,1,0:T(8,128)(2,1)S(1)}, u32[]{:S(2)}, u32[]{:S(2)}) async-start(bf16[8,18,1024]{2,1,0:T(8,128)(2,1)} %fusion.22), calls=%async_computation.1 | async-start | bytes 786432 | tf_op jit(solution)/shard_map/all_to_all | solution.py:167
  440.1 11.7 %all-to-all-done.1 = bf16[8,18,1024]{2,1,0:T(8,128)(2,1)S(1)} async-done(((bf16[8,18,1024]{2,1,0:T(8,128)(2,1)}), bf16[8,18,1024]{2,1,0:T(8,128)(2,1)S(1)}, u32[]{:S(2)}, u32[]{:S(2)}) %all-to-all-start.1) | async-done | bytes 294944 | tf_op jit(solution)/shard_map/all_to_all | solution.py:167
  451.9 0.8 gather_fusion
  453.0 0.8 multiply_reduce_fusion.1
  (69 shorter events, 7.7 us)
Async XLA Ops:
  6.5 433.2 %copy-start = (bf16[4096,8]{0,1:T(8,128)(2,1)S(1)}, bf16[4096,8]{0,1:T(8,128)(2,1)}, u32[]{:S(2)}) copy-start(bf16[4096,8]{0,1:T(8,128)(2,1)} %param.27) | copy-start | bytes 196612
  6.5 22.9 %copy-start.5 = (s32[1,64]{1,0:T(1,128)S(1)}, s32[1,64]{1,0:T(1,128)}, u32[]{:S(2)}) copy-start(s32[1,64]{1,0:T(1,128)} %param.25) | copy-start | bytes 772
  6.5 58.7 %all-gather.7.cloned.1.call-start = ((), (), s32[]{:S(2)}) async-start(), calls=%async_computation.3 | async-start | bytes 1179648 | tf_op jit(solution)/shard_map/all_gather | solution.py:129
  7.3 174.3 %all-gather.5.cloned.1.call-start = ((), (), s32[]{:S(2)}) async-start(), calls=%async_computation.2 | async-start | bytes 1179648 | tf_op jit(solution)/shard_map/all_gather | solution.py:130
  8.0 247.9 %all-gather.9.cloned.1.call-start = ((), (), s32[]{:S(2)}) async-start(), calls=%async_computation.4 | async-start | bytes 4718592 | tf_op jit(solution)/shard_map/all_gather | solution.py:128
  8.7 292.7 %all-reduce.2.cloned.1.call-start = ((), (), s32[]{:S(2)}) async-start(), calls=%async_computation.5 | async-start | bytes 2097152 | tf_op jit(solution)/shard_map/psum | solution.py:145
  8.8 16.6 %collective-permute-start = (bf16[512,512]{1,0:T(8,128)(2,1)}, bf16[512,512]{1,0:T(8,128)(2,1)S(1)}, u32[]{:S(2)}, u32[]{:S(2)}) collective-permute-start(bf16[512,512]{1,0:T(8,128)(2,1)} %param.21), channel_id=1, source_target_pairs={{0,1},{1,0},{2,3},{3,2},{4,5},{5,4},{6,7},{7,6},{8,9},{9,8},{10,11... | collective-permute-start | bytes 1572872 | tf_op jit(solution)/shard_map/ppermute | solution.py:117
  26.9 34.2 %collective-permute-start.1 = (bf16[512,1024]{1,0:T(8,128)(2,1)S(1)}, bf16[512,1024]{1,0:T(8,128)(2,1)S(1)}, u32[]{:S(2)}, u32[]{:S(2)}) collective-permute-start(bf16[512,1024]{1,0:T(8,128)(2,1)S(1)} %maximum_select_fusion.3), channel_id=1, source_target_pairs={{0,2},{1,3},{2,0},{3,1},{4,6},{5,7},{6,4},{7,5},{8,10},{9,11},{10,... | collective-permute-start | bytes 3145736 | tf_op jit(solution)/shard_map/ppermute | solution.py:117
  29.6 35.7 %copy-start.1 = (bf16[64,4096]{1,0:T(8,128)(2,1)S(1)}, bf16[64,4096]{1,0:T(8,128)(2,1)}, u32[]{:S(2)}) copy-start(bf16[64,4096]{1,0:T(8,128)(2,1)} %param.16) | copy-start | bytes 1572868
  29.6 35.7 %copy-start.2 = (f32[4096]{0:T(1024)S(1)}, f32[4096]{0:T(1024)}, u32[]{:S(2)}) copy-start(f32[4096]{0:T(1024)} %param.17) | copy-start | bytes 49156
  63.2 197.9 %collective-permute-start.2 = (bf16[512,2048]{1,0:T(8,128)(2,1)}, bf16[512,2048]{1,0:T(8,128)(2,1)}, u32[]{:S(2)}, u32[]{:S(2)}) collective-permute-start(bf16[512,2048]{1,0:T(8,128)(2,1)} %maximum_select_fusion.2), channel_id=1, source_target_pairs={{0,4},{1,5},{2,6},{3,7},{4,0},{5,1},{6,2},{7,3},{8,12},{9,13},{10,... | collective-permute-start | bytes 6291464 | tf_op jit(solution)/shard_map/ppermute | solution.py:117
  183.3 76.1 %copy-start.6 = (bf16[8,256,128]{2,1,0:T(8,128)(2,1)S(1)}, bf16[8,256,128]{2,1,0:T(8,128)(2,1)}, u32[]{:S(2)}) copy-start(bf16[8,256,128]{2,1,0:T(8,128)(2,1)} %param.22) | copy-start | bytes 1572868
  259.4 1.1 copy-start.7
  267.0 36.0 %copy-start.3 = (f32[4096]{0:T(1024)S(1)}, f32[4096]{0:T(1024)}, u32[]{:S(2)}) copy-start(f32[4096]{0:T(1024)} %param.26) | copy-start | bytes 49156
  267.0 152.5 %all-gather.11.cloned.1.call-start = ((), (), s32[]{:S(2)}) async-start(), calls=%async_computation.6 | async-start | bytes 6881280 | tf_op jit(solution)/shard_map/all_gather | solution.py:162
  365.2 13.7 %copy-start.4 = (s32[64,2]{0,1:T(2,128)S(1)}, s32[64,2]{0,1:T(2,128)}, u32[]{:S(2)}) copy-start(s32[64,2]{0,1:T(2,128)} %param.28) | copy-start | bytes 1540
  434.2 17.6 %all-to-all-start.1 = ((bf16[8,18,1024]{2,1,0:T(8,128)(2,1)}), bf16[8,18,1024]{2,1,0:T(8,128)(2,1)S(1)}, u32[]{:S(2)}, u32[]{:S(2)}) async-start(bf16[8,18,1024]{2,1,0:T(8,128)(2,1)} %fusion.22), calls=%async_computation.1 | async-start | bytes 786432 | tf_op jit(solution)/shard_map/all_to_all | solution.py:167
Sparse Core Ops, SparseCore 0:
  9.5 47.2 all-gather.6
  58.9 122.6 all-gather.4
  183.7 72.1 all-gather.8
  267.1 34.3 all-reduce.1
  378.8 40.6 all-gather.10
